TPU v7x, 128 devices: a whole 4x4x4 slice. The times are simulated.
128 devices in a mesh: stream: 16 (over y, x), azim: 8 (over z, core).
Axes of the slice: x: 4, y: 4, z: 4, core: 2. Of those that a mesh axis runs over, the one named last changes fastest.
Arguments:
- start_vector: bfloat16 [64, 8, 8, 64, 128], P('stream', 'azim'), may hold values from -6 to 6
- trace_blocks: bfloat16 [64, 8, 8, 64, 768], P('stream', 'azim'), may hold values from -0.21875 to 0.21875
- neighbour: int32 [8, 8, 12], P('azim'), may hold values from 0 to 71
Outputs:
- krylov_basis: bfloat16 [4, 64, 8, 8, 64, 128], P(None, 'stream', 'azim')
Inputs may be any that keep to these rules, and one draw needn't show every extreme that they name: `neighbour`: entry e names column offsets (e // 24 - 1, (e // 8) % 3 - 1) and slot e % 8; the list is the same for every stream column.
All inputs are finite; a program needn't handle non-finite values.
Results may differ from a plain program's by a relative error of at most 0.0055.
Values may be sent and summed in bfloat16 or wider, within the bound.
A program may use at most 64 MiB of HBM per device.

v0:
```python
import jax
import jax.numpy as jnp
from jax import lax
from jax.sharding import PartitionSpec as P

STEPS = 4


def with_halo(block, sides, width):
    for axis, dim in sides:
        count = lax.axis_size(axis)
        forward = [(i, i + 1) for i in range(count - 1)]
        forward.append((count - 1, 0))
        backward = [(target, source) for source, target in forward]
        low = lax.ppermute(
            lax.slice_in_dim(block, block.shape[dim] - width, None, axis=dim), axis, forward
        )
        high = lax.ppermute(lax.slice_in_dim(block, 0, width, axis=dim), axis, backward)
        block = jnp.concatenate([low, block, high], axis=dim)
    return block


def apply_rows(padded, blocks, neighbour, rows):
    column_count = padded.shape[1] - 2
    face_count = padded.shape[2]
    width = padded.shape[3]
    rhs_count = padded.shape[4]
    pieces = []
    for stream_shift in range(3):
        for azim_shift in range(3):
            pieces.append(
                padded[stream_shift : stream_shift + rows, azim_shift : azim_shift + column_count]
            )
    window = jnp.stack(pieces, axis=2)
    window = window.reshape(rows, column_count, 9 * face_count, width * rhs_count)
    codes = jnp.arange(9 * face_count, dtype=jnp.int32)
    selector = (neighbour.reshape(column_count, -1)[:, :, None] == codes[None, None, :]).astype(
        jnp.bfloat16
    )
    gathered = jnp.einsum("jtq,ijqx->ijtx", selector, window, preferred_element_type=jnp.float32)
    gathered = gathered.astype(jnp.bfloat16)
    gathered = gathered.reshape(rows, column_count, face_count, -1, rhs_count)
    product = jnp.einsum("ijcam,ijcmr->ijcar", blocks, gathered, preferred_element_type=jnp.float32)
    return product.astype(jnp.bfloat16)


def local(start_vector, trace_blocks, neighbour):
    own_columns = start_vector.shape[0]
    basis = []
    current = start_vector
    for layer_index in range(STEPS):
        padded = with_halo(current, (("stream", 0), ("azim", 1)), 1)
        current = apply_rows(padded, trace_blocks, neighbour, own_columns)
        basis.append(current)
    return jnp.stack(basis)


def solution(mesh):
    return jax.shard_map(
        local,
        mesh=mesh,
        in_specs=(
            P("stream", "azim", None, None, None),
            P("stream", "azim", None, None, None),
            P("azim", None, None),
        ),
        out_specs=P(None, "stream", "azim", None, None, None),
        check_vma=False,
    )
```

profile of v0, /device:TPU:0, one launch (start us, length us, event | category | flops | bytes accessed | tf_op | source)
XLA Modules:
  0.0 228.5 jit_solution(7378601925938237684)
XLA Ops:
  2.8 3.8 %collective-permute-start.1 = (bf16[1,1,8,64,128]{4,3,2,0,1:T(8,128)(2,1)S(1)}, bf16[1,1,8,64,128]{4,3,2,0,1:T(8,128)(2,1)S(1)}, u32[]{:S(2)}, u32[]{:S(2)}) collective-permute-start(bf16[1,1,8,64,128]{4,3,2,0,1:T(8,128)(2,1)S(1)} %get-tuple-element.12), channel_id=1, source_target_pairs={{8,0},{16,8},{24,16},{32,24},{40,32},{48,40},{56,48},{64,56},{72,6... | collective-permute-start | bytes 393224 | tf_op jit(solution)/shard_map/ppermute | solution.py:18
  6.6 3.4 %collective-permute-done = bf16[1,1,8,64,128]{4,3,2,0,1:T(8,128)(2,1)S(1)} collective-permute-done((bf16[1,1,8,64,128]{4,3,2,0,1:T(8,128)(2,1)S(1)}, bf16[1,1,8,64,128]{4,3,2,0,1:T(8,128)(2,1)S(1)}, u32[]{:S(2)}, u32[]{:S(2)}) %collective-permute-start) | collective-permute-done | bytes 131104 | tf_op jit(solution)/shard_map/ppermute | solution.py:15
  12.1 3.0 %collective-permute-start.3 = (bf16[6,1,8,64,128]{4,3,2,0,1:T(8,128)(2,1)}, bf16[6,1,8,64,128]{4,3,2,0,1:T(8,128)(2,1)}, u32[]{:S(2)}, u32[]{:S(2)}) collective-permute-start(bf16[6,1,8,64,128]{4,3,2,0,1:T(8,128)(2,1)} %pad_maximum_fusion), channel_id=1, source_target_pairs={{1,0},{2,1},{3,2},{4,3},{5,4},{6,5},{7,6},{0,7},{9,8},{10,9},{11,1... | collective-permute-start | bytes 2359304 | tf_op jit(solution)/shard_map/ppermute | solution.py:18
  15.8 9.2 %collective-permute-done.2 = bf16[6,1,8,64,128]{4,3,2,0,1:T(8,128)(2,1)} collective-permute-done((bf16[6,1,8,64,128]{4,3,2,0,1:T(8,128)(2,1)}, bf16[6,1,8,64,128]{4,3,2,0,1:T(8,128)(2,1)}, u32[]{:S(2)}, u32[]{:S(2)}) %collective-permute-start.2) | collective-permute-done | bytes 786464 | tf_op jit(solution)/shard_map/ppermute | solution.py:15
  33.9 13.1 %fusion = bf16[4,1,96,8192]{3,2,0,1:T(8,128)(2,1)} fusion(bf16[4,1,9,8,64,128]{5,4,3,0,2,1:T(8,128)(2,1)S(1)} %fusion.59, s32[96]{0:T(128)S(1)} %eq.69), kind=kOutput, calls=%fused_computation.4 | convolution fusion | flops 456137472 | bytes 11010432 | tf_op jit(solution)/shard_map/jtq,ijqx->ijtx/dot_general | solution.py:40
  47.1 10.5 %reshape.187 = bf16[4,8,768,128]{3,2,1,0:T(8,128)(2,1)} reshape(bf16[4,1,96,8192]{3,2,0,1:T(8,128)(2,1)} %fusion) | data formatting | bytes 12582912 | tf_op jit(solution)/shard_map/reshape.6
  57.6 4.1 %fusion.23 = bf16[4,8,128,64]{2,3,1,0:T(8,128)(2,1)S(1)} fusion(bf16[4,8,768,128]{3,2,1,0:T(8,128)(2,1)} %reshape.187, bf16[4,1,8,64,768]{4,3,2,1,0:T(8,128)(2,1)S(1)} %copy-done), kind=kOutput, calls=%fused_computation.22 | convolution fusion | flops 402915328 | bytes 9961472 | tf_op jit(solution)/shard_map/ijcam,ijcmr->ijcar/dot_general | solution.py:43
  61.8 5.3 %collective-permute-start.5 = (bf16[1,1,8,64,128]{4,3,2,0,1:T(8,128)(2,1)S(1)}, bf16[1,1,8,64,128]{4,3,2,0,1:T(8,128)(2,1)S(1)}, u32[]{:S(2)}, u32[]{:S(2)}) collective-permute-start(bf16[1,1,8,64,128]{4,3,2,0,1:T(8,128)(2,1)S(1)} %get-tuple-element.10), channel_id=1, source_target_pairs={{8,0},{16,8},{24,16},{32,24},{40,32},{48,40},{56,48},{64,56},{72,6... | collective-permute-start | bytes 393224 | tf_op jit(solution)/shard_map/ppermute | solution.py:18
  70.2 2.9 %collective-permute-start.7 = (bf16[6,1,8,64,128]{4,3,2,0,1:T(8,128)(2,1)S(1)}, bf16[6,1,8,64,128]{4,3,2,0,1:T(8,128)(2,1)S(1)}, u32[]{:S(2)}, u32[]{:S(2)}) collective-permute-start(bf16[6,1,8,64,128]{4,3,2,0,1:T(8,128)(2,1)S(1)} %pad_maximum_fusion.1), channel_id=1, source_target_pairs={{1,0},{2,1},{3,2},{4,3},{5,4},{6,5},{7,6},{0,7},{9,8},{10,9},{11,1... | collective-permute-start | bytes 2359304 | tf_op jit(solution)/shard_map/ppermute | solution.py:18
  73.2 9.7 %collective-permute-done.6 = bf16[6,1,8,64,128]{4,3,2,0,1:T(8,128)(2,1)S(1)} collective-permute-done((bf16[6,1,8,64,128]{4,3,2,0,1:T(8,128)(2,1)S(1)}, bf16[6,1,8,64,128]{4,3,2,0,1:T(8,128)(2,1)S(1)}, u32[]{:S(2)}, u32[]{:S(2)}) %collective-permute-start.6) | collective-permute-done | bytes 786464 | tf_op jit(solution)/shard_map/ppermute | solution.py:15
  83.5 3.2 %copy.17 = bf16[4,1,9,8,64,128]{5,4,3,2,0,1:T(8,128)(2,1)} copy(bf16[4,1,9,8,64,128]{5,4,3,0,2,1:T(8,128)(2,1)S(1)} %fusion.49) | data formatting | bytes 9437184 | tf_op jit(solution)/shard_map/stack | solution.py:34
  86.7 8.2 %reshape.189 = bf16[4,72,8192]{2,1,0:T(8,128)(2,1)} reshape(bf16[4,1,9,8,64,128]{5,4,3,2,0,1:T(8,128)(2,1)} %copy.17) | data formatting | bytes 9437184 | tf_op jit(solution)/shard_map/reshape.16
  94.9 6.9 %fusion.1 = bf16[4,1,96,8192]{3,2,0,1:T(8,128)(2,1)} fusion(bf16[4,72,8192]{2,1,0:T(8,128)(2,1)} %reshape.189, s32[96]{0:T(128)S(1)} %eq.69), kind=kOutput, calls=%fused_computation.5 | convolution fusion | flops 456137472 | bytes 11010432 | tf_op jit(solution)/shard_map/jtq,ijqx->ijtx/dot_general | solution.py:40
  101.9 10.5 %reshape.190 = bf16[4,8,768,128]{3,2,1,0:T(8,128)(2,1)} reshape(bf16[4,1,96,8192]{3,2,0,1:T(8,128)(2,1)} %fusion.1) | data formatting | bytes 12582912 | tf_op jit(solution)/shard_map/reshape.20
  112.4 4.1 %fusion.20 = bf16[4,8,128,64]{2,3,1,0:T(8,128)(2,1)S(1)} fusion(bf16[4,8,768,128]{3,2,1,0:T(8,128)(2,1)} %reshape.190, bf16[4,1,8,64,768]{4,3,2,1,0:T(8,128)(2,1)S(1)} %copy-done), kind=kOutput, calls=%fused_computation.21 | convolution fusion | flops 402915328 | bytes 9961472 | tf_op jit(solution)/shard_map/ijcam,ijcmr->ijcar/dot_general | solution.py:43
  116.6 5.4 %collective-permute-start.9 = (bf16[1,1,8,64,128]{4,3,2,0,1:T(8,128)(2,1)S(1)}, bf16[1,1,8,64,128]{4,3,2,0,1:T(8,128)(2,1)S(1)}, u32[]{:S(2)}, u32[]{:S(2)}) collective-permute-start(bf16[1,1,8,64,128]{4,3,2,0,1:T(8,128)(2,1)S(1)} %get-tuple-element.8), channel_id=1, source_target_pairs={{8,0},{16,8},{24,16},{32,24},{40,32},{48,40},{56,48},{64,56},{72,6... | collective-permute-start | bytes 393224 | tf_op jit(solution)/shard_map/ppermute | solution.py:18
  122.0 3.5 %collective-permute-done.8 = bf16[1,1,8,64,128]{4,3,2,0,1:T(8,128)(2,1)S(1)} collective-permute-done((bf16[1,1,8,64,128]{4,3,2,0,1:T(8,128)(2,1)S(1)}, bf16[1,1,8,64,128]{4,3,2,0,1:T(8,128)(2,1)S(1)}, u32[]{:S(2)}, u32[]{:S(2)}) %collective-permute-start.8) | collective-permute-done | bytes 131104 | tf_op jit(solution)/shard_map/ppermute | solution.py:15
  125.7 2.9 %collective-permute-start.11 = (bf16[6,1,8,64,128]{4,3,2,0,1:T(8,128)(2,1)S(1)}, bf16[6,1,8,64,128]{4,3,2,0,1:T(8,128)(2,1)S(1)}, u32[]{:S(2)}, u32[]{:S(2)}) collective-permute-start(bf16[6,1,8,64,128]{4,3,2,0,1:T(8,128)(2,1)S(1)} %pad_maximum_fusion.2), channel_id=1, source_target_pairs={{1,0},{2,1},{3,2},{4,3},{5,4},{6,5},{7,6},{0,7},{9,8},{10,9},{11,1... | collective-permute-start | bytes 2359304 | tf_op jit(solution)/shard_map/ppermute | solution.py:18
  128.6 9.7 %collective-permute-done.10 = bf16[6,1,8,64,128]{4,3,2,0,1:T(8,128)(2,1)S(1)} collective-permute-done((bf16[6,1,8,64,128]{4,3,2,0,1:T(8,128)(2,1)S(1)}, bf16[6,1,8,64,128]{4,3,2,0,1:T(8,128)(2,1)S(1)}, u32[]{:S(2)}, u32[]{:S(2)}) %collective-permute-start.10) | collective-permute-done | bytes 786464 | tf_op jit(solution)/shard_map/ppermute | solution.py:15
  139.0 3.2 %copy.18 = bf16[4,1,9,8,64,128]{5,4,3,2,0,1:T(8,128)(2,1)} copy(bf16[4,1,9,8,64,128]{5,4,3,0,2,1:T(8,128)(2,1)S(1)} %fusion.39) | data formatting | bytes 9437184 | tf_op jit(solution)/shard_map/stack | solution.py:34
  142.2 8.2 %reshape.191 = bf16[4,72,8192]{2,1,0:T(8,128)(2,1)} reshape(bf16[4,1,9,8,64,128]{5,4,3,2,0,1:T(8,128)(2,1)} %copy.18) | data formatting | bytes 9437184 | tf_op jit(solution)/shard_map/reshape.22
  150.4 6.9 %fusion.2 = bf16[4,1,96,8192]{3,2,0,1:T(8,128)(2,1)} fusion(bf16[4,72,8192]{2,1,0:T(8,128)(2,1)} %reshape.191, s32[96]{0:T(128)S(1)} %eq.69), kind=kOutput, calls=%fused_computation.6 | convolution fusion | flops 456137472 | bytes 11010432 | tf_op jit(solution)/shard_map/jtq,ijqx->ijtx/dot_general | solution.py:40
  157.3 10.5 %reshape.192 = bf16[4,8,768,128]{3,2,1,0:T(8,128)(2,1)} reshape(bf16[4,1,96,8192]{3,2,0,1:T(8,128)(2,1)} %fusion.2) | data formatting | bytes 12582912 | tf_op jit(solution)/shard_map/reshape.26
  167.8 4.1 %fusion.17 = bf16[4,8,128,64]{2,3,1,0:T(8,128)(2,1)S(1)} fusion(bf16[4,8,768,128]{3,2,1,0:T(8,128)(2,1)} %reshape.192, bf16[4,1,8,64,768]{4,3,2,1,0:T(8,128)(2,1)S(1)} %copy-done), kind=kOutput, calls=%fused_computation.20 | convolution fusion | flops 402915328 | bytes 9961472 | tf_op jit(solution)/shard_map/ijcam,ijcmr->ijcar/dot_general | solution.py:43
  172.1 5.3 %collective-permute-start.13 = (bf16[1,1,8,64,128]{4,3,2,0,1:T(8,128)(2,1)S(1)}, bf16[1,1,8,64,128]{4,3,2,0,1:T(8,128)(2,1)S(1)}, u32[]{:S(2)}, u32[]{:S(2)}) collective-permute-start(bf16[1,1,8,64,128]{4,3,2,0,1:T(8,128)(2,1)S(1)} %get-tuple-element.6), channel_id=1, source_target_pairs={{8,0},{16,8},{24,16},{32,24},{40,32},{48,40},{56,48},{64,56},{72,6... | collective-permute-start | bytes 393224 | tf_op jit(solution)/shard_map/ppermute | solution.py:18
  180.5 2.9 %collective-permute-start.15 = (bf16[6,1,8,64,128]{4,3,2,0,1:T(8,128)(2,1)S(1)}, bf16[6,1,8,64,128]{4,3,2,0,1:T(8,128)(2,1)S(1)}, u32[]{:S(2)}, u32[]{:S(2)}) collective-permute-start(bf16[6,1,8,64,128]{4,3,2,0,1:T(8,128)(2,1)S(1)} %pad_maximum_fusion.3), channel_id=1, source_target_pairs={{1,0},{2,1},{3,2},{4,3},{5,4},{6,5},{7,6},{0,7},{9,8},{10,9},{11,1... | collective-permute-start | bytes 2359304 | tf_op jit(solution)/shard_map/ppermute | solution.py:18
  183.4 9.7 %collective-permute-done.14 = bf16[6,1,8,64,128]{4,3,2,0,1:T(8,128)(2,1)S(1)} collective-permute-done((bf16[6,1,8,64,128]{4,3,2,0,1:T(8,128)(2,1)S(1)}, bf16[6,1,8,64,128]{4,3,2,0,1:T(8,128)(2,1)S(1)}, u32[]{:S(2)}, u32[]{:S(2)}) %collective-permute-start.14) | collective-permute-done | bytes 786464 | tf_op jit(solution)/shard_map/ppermute | solution.py:15
  193.8 3.2 %copy.19 = bf16[4,1,9,8,64,128]{5,4,3,2,0,1:T(8,128)(2,1)} copy(bf16[4,1,9,8,64,128]{5,4,3,0,2,1:T(8,128)(2,1)S(1)} %fusion.29) | data formatting | bytes 9437184 | tf_op jit(solution)/shard_map/stack | solution.py:34
  197.0 8.2 %reshape.193 = bf16[4,72,8192]{2,1,0:T(8,128)(2,1)} reshape(bf16[4,1,9,8,64,128]{5,4,3,2,0,1:T(8,128)(2,1)} %copy.19) | data formatting | bytes 9437184 | tf_op jit(solution)/shard_map/reshape.28
  205.2 6.9 %fusion.3 = bf16[4,1,96,8192]{3,2,0,1:T(8,128)(2,1)} fusion(bf16[4,72,8192]{2,1,0:T(8,128)(2,1)} %reshape.193, s32[96]{0:T(128)S(1)} %eq.69), kind=kOutput, calls=%fused_computation.7 | convolution fusion | flops 456137472 | bytes 11010432 | tf_op jit(solution)/shard_map/jtq,ijqx->ijtx/dot_general | solution.py:40
  212.1 10.5 %reshape.194 = bf16[4,8,768,128]{3,2,1,0:T(8,128)(2,1)} reshape(bf16[4,1,96,8192]{3,2,0,1:T(8,128)(2,1)} %fusion.3) | data formatting | bytes 12582912 | tf_op jit(solution)/shard_map/reshape.32
  222.6 4.2 %fusion.26 = bf16[1,4,1,8,64,128]{5,4,3,1,2,0:T(8,128)(2,1)S(1)} fusion(bf16[4,8,768,128]{3,2,1,0:T(8,128)(2,1)} %reshape.194, bf16[4,1,8,64,768]{4,3,2,1,0:T(8,128)(2,1)S(1)} %copy-done), kind=kOutput, calls=%fused_computation.23 | convolution fusion | flops 402915328 | bytes 9961472 | tf_op jit(solution)/shard_map/ijcam,ijcmr->ijcar/dot_general | solution.py:43
  (80 shorter events, 24.4 us)
Async XLA Ops:
  0.0 57.6 %copy-start = (bf16[4,1,8,64,768]{4,3,2,1,0:T(8,128)(2,1)S(1)}, bf16[4,1,8,64,768]{4,3,2,1,0:T(8,128)(2,1)}, u32[]{:S(2)}) copy-start(bf16[4,1,8,64,768]{4,3,2,1,0:T(8,128)(2,1)} %param.4) | copy-start | bytes 9437188
  1.1 8.9 %collective-permute-start = (bf16[1,1,8,64,128]{4,3,2,0,1:T(8,128)(2,1)S(1)}, bf16[1,1,8,64,128]{4,3,2,0,1:T(8,128)(2,1)S(1)}, u32[]{:S(2)}, u32[]{:S(2)}) collective-permute-start(bf16[1,1,8,64,128]{4,3,2,0,1:T(8,128)(2,1)S(1)} %get-tuple-element.11), channel_id=1, source_target_pairs={{0,8},{8,16},{16,24},{24,32},{32,40},{40,48},{48,56},{56,64},{64,7... | collective-permute-start | bytes 393224 | tf_op jit(solution)/shard_map/ppermute | solution.py:15
  2.8 7.2 %collective-permute-start.1 = (bf16[1,1,8,64,128]{4,3,2,0,1:T(8,128)(2,1)S(1)}, bf16[1,1,8,64,128]{4,3,2,0,1:T(8,128)(2,1)S(1)}, u32[]{:S(2)}, u32[]{:S(2)}) collective-permute-start(bf16[1,1,8,64,128]{4,3,2,0,1:T(8,128)(2,1)S(1)} %get-tuple-element.12), channel_id=1, source_target_pairs={{8,0},{16,8},{24,16},{32,24},{40,32},{48,40},{56,48},{64,56},{72,6... | collective-permute-start | bytes 393224 | tf_op jit(solution)/shard_map/ppermute | solution.py:18
  12.0 12.9 %collective-permute-start.2 = (bf16[6,1,8,64,128]{4,3,2,0,1:T(8,128)(2,1)}, bf16[6,1,8,64,128]{4,3,2,0,1:T(8,128)(2,1)}, u32[]{:S(2)}, u32[]{:S(2)}) collective-permute-start(bf16[6,1,8,64,128]{4,3,2,0,1:T(8,128)(2,1)} %pad_maximum_fusion), channel_id=1, source_target_pairs={{0,1},{1,2},{2,3},{3,4},{4,5},{5,6},{6,7},{7,0},{8,9},{9,10},{10,1... | collective-permute-start | bytes 2359304 | tf_op jit(solution)/shard_map/ppermute | solution.py:15
  12.1 15.1 %collective-permute-start.3 = (bf16[6,1,8,64,128]{4,3,2,0,1:T(8,128)(2,1)}, bf16[6,1,8,64,128]{4,3,2,0,1:T(8,128)(2,1)}, u32[]{:S(2)}, u32[]{:S(2)}) collective-permute-start(bf16[6,1,8,64,128]{4,3,2,0,1:T(8,128)(2,1)} %pad_maximum_fusion), channel_id=1, source_target_pairs={{1,0},{2,1},{3,2},{4,3},{5,4},{6,5},{7,6},{0,7},{9,8},{10,9},{11,1... | collective-permute-start | bytes 2359304 | tf_op jit(solution)/shard_map/ppermute | solution.py:18
  15.8 17.0 %copy-start.7 = (bf16[4,1,8,64,128]{4,3,2,1,0:T(8,128)(2,1)S(1)}, bf16[4,1,8,64,128]{4,3,2,1,0:T(8,128)(2,1)}, u32[]{:S(2)}) copy-start(bf16[4,1,8,64,128]{4,3,2,1,0:T(8,128)(2,1)} %param.3) | copy-start | bytes 1572868
  61.7 21.7 %copy-start.1 = (bf16[4,8,128,64]{2,3,1,0:T(8,128)(2,1)}, bf16[4,8,128,64]{2,3,1,0:T(8,128)(2,1)S(1)}, u32[]{:S(2)}) copy-start(bf16[4,8,128,64]{2,3,1,0:T(8,128)(2,1)S(1)} %fusion.23) | copy-start | bytes 1572868
  61.7 8.4 %collective-permute-start.4 = (bf16[1,1,8,64,128]{4,3,2,0,1:T(8,128)(2,1)S(1)}, bf16[1,1,8,64,128]{4,3,2,0,1:T(8,128)(2,1)S(1)}, u32[]{:S(2)}, u32[]{:S(2)}) collective-permute-start(bf16[1,1,8,64,128]{4,3,2,0,1:T(8,128)(2,1)S(1)} %get-tuple-element.9), channel_id=1, source_target_pairs={{0,8},{8,16},{16,24},{24,32},{32,40},{40,48},{48,56},{56,64},{64,7... | collective-permute-start | bytes 393224 | tf_op jit(solution)/shard_map/ppermute | solution.py:15
  61.8 8.3 %collective-permute-start.5 = (bf16[1,1,8,64,128]{4,3,2,0,1:T(8,128)(2,1)S(1)}, bf16[1,1,8,64,128]{4,3,2,0,1:T(8,128)(2,1)S(1)}, u32[]{:S(2)}, u32[]{:S(2)}) collective-permute-start(bf16[1,1,8,64,128]{4,3,2,0,1:T(8,128)(2,1)S(1)} %get-tuple-element.10), channel_id=1, source_target_pairs={{8,0},{16,8},{24,16},{32,24},{40,32},{48,40},{56,48},{64,56},{72,6... | collective-permute-start | bytes 393224 | tf_op jit(solution)/shard_map/ppermute | solution.py:18
  70.2 12.6 %collective-permute-start.6 = (bf16[6,1,8,64,128]{4,3,2,0,1:T(8,128)(2,1)S(1)}, bf16[6,1,8,64,128]{4,3,2,0,1:T(8,128)(2,1)S(1)}, u32[]{:S(2)}, u32[]{:S(2)}) collective-permute-start(bf16[6,1,8,64,128]{4,3,2,0,1:T(8,128)(2,1)S(1)} %pad_maximum_fusion.1), channel_id=1, source_target_pairs={{0,1},{1,2},{2,3},{3,4},{4,5},{5,6},{6,7},{7,0},{8,9},{9,10},{10,1... | collective-permute-start | bytes 2359304 | tf_op jit(solution)/shard_map/ppermute | solution.py:15
  70.2 12.7 %collective-permute-start.7 = (bf16[6,1,8,64,128]{4,3,2,0,1:T(8,128)(2,1)S(1)}, bf16[6,1,8,64,128]{4,3,2,0,1:T(8,128)(2,1)S(1)}, u32[]{:S(2)}, u32[]{:S(2)}) collective-permute-start(bf16[6,1,8,64,128]{4,3,2,0,1:T(8,128)(2,1)S(1)} %pad_maximum_fusion.1), channel_id=1, source_target_pairs={{1,0},{2,1},{3,2},{4,3},{5,4},{6,5},{7,6},{0,7},{9,8},{10,9},{11,1... | collective-permute-start | bytes 2359304 | tf_op jit(solution)/shard_map/ppermute | solution.py:18
  116.5 22.3 %copy-start.3 = (bf16[4,8,128,64]{2,3,1,0:T(8,128)(2,1)}, bf16[4,8,128,64]{2,3,1,0:T(8,128)(2,1)S(1)}, u32[]{:S(2)}) copy-start(bf16[4,8,128,64]{2,3,1,0:T(8,128)(2,1)S(1)} %fusion.20) | copy-start | bytes 1572868
  116.5 9.0 %collective-permute-start.8 = (bf16[1,1,8,64,128]{4,3,2,0,1:T(8,128)(2,1)S(1)}, bf16[1,1,8,64,128]{4,3,2,0,1:T(8,128)(2,1)S(1)}, u32[]{:S(2)}, u32[]{:S(2)}) collective-permute-start(bf16[1,1,8,64,128]{4,3,2,0,1:T(8,128)(2,1)S(1)} %get-tuple-element.7), channel_id=1, source_target_pairs={{0,8},{8,16},{16,24},{24,32},{32,40},{40,48},{48,56},{56,64},{64,7... | collective-permute-start | bytes 393224 | tf_op jit(solution)/shard_map/ppermute | solution.py:15
  116.6 8.9 %collective-permute-start.9 = (bf16[1,1,8,64,128]{4,3,2,0,1:T(8,128)(2,1)S(1)}, bf16[1,1,8,64,128]{4,3,2,0,1:T(8,128)(2,1)S(1)}, u32[]{:S(2)}, u32[]{:S(2)}) collective-permute-start(bf16[1,1,8,64,128]{4,3,2,0,1:T(8,128)(2,1)S(1)} %get-tuple-element.8), channel_id=1, source_target_pairs={{8,0},{16,8},{24,16},{32,24},{40,32},{48,40},{56,48},{64,56},{72,6... | collective-permute-start | bytes 393224 | tf_op jit(solution)/shard_map/ppermute | solution.py:18
  125.6 12.6 %collective-permute-start.10 = (bf16[6,1,8,64,128]{4,3,2,0,1:T(8,128)(2,1)S(1)}, bf16[6,1,8,64,128]{4,3,2,0,1:T(8,128)(2,1)S(1)}, u32[]{:S(2)}, u32[]{:S(2)}) collective-permute-start(bf16[6,1,8,64,128]{4,3,2,0,1:T(8,128)(2,1)S(1)} %pad_maximum_fusion.2), channel_id=1, source_target_pairs={{0,1},{1,2},{2,3},{3,4},{4,5},{5,6},{6,7},{7,0},{8,9},{9,10},{10,1... | collective-permute-start | bytes 2359304 | tf_op jit(solution)/shard_map/ppermute | solution.py:15
  125.7 12.7 %collective-permute-start.11 = (bf16[6,1,8,64,128]{4,3,2,0,1:T(8,128)(2,1)S(1)}, bf16[6,1,8,64,128]{4,3,2,0,1:T(8,128)(2,1)S(1)}, u32[]{:S(2)}, u32[]{:S(2)}) collective-permute-start(bf16[6,1,8,64,128]{4,3,2,0,1:T(8,128)(2,1)S(1)} %pad_maximum_fusion.2), channel_id=1, source_target_pairs={{1,0},{2,1},{3,2},{4,3},{5,4},{6,5},{7,6},{0,7},{9,8},{10,9},{11,1... | collective-permute-start | bytes 2359304 | tf_op jit(solution)/shard_map/ppermute | solution.py:18
  171.9 21.7 %copy-start.5 = (bf16[4,8,128,64]{2,3,1,0:T(8,128)(2,1)}, bf16[4,8,128,64]{2,3,1,0:T(8,128)(2,1)S(1)}, u32[]{:S(2)}) copy-start(bf16[4,8,128,64]{2,3,1,0:T(8,128)(2,1)S(1)} %fusion.17) | copy-start | bytes 1572868
  172.0 8.4 %collective-permute-start.12 = (bf16[1,1,8,64,128]{4,3,2,0,1:T(8,128)(2,1)S(1)}, bf16[1,1,8,64,128]{4,3,2,0,1:T(8,128)(2,1)S(1)}, u32[]{:S(2)}, u32[]{:S(2)}) collective-permute-start(bf16[1,1,8,64,128]{4,3,2,0,1:T(8,128)(2,1)S(1)} %get-tuple-element.5), channel_id=1, source_target_pairs={{0,8},{8,16},{16,24},{24,32},{32,40},{40,48},{48,56},{56,64},{64,7... | collective-permute-start | bytes 393224 | tf_op jit(solution)/shard_map/ppermute | solution.py:15
  172.1 8.3 %collective-permute-start.13 = (bf16[1,1,8,64,128]{4,3,2,0,1:T(8,128)(2,1)S(1)}, bf16[1,1,8,64,128]{4,3,2,0,1:T(8,128)(2,1)S(1)}, u32[]{:S(2)}, u32[]{:S(2)}) collective-permute-start(bf16[1,1,8,64,128]{4,3,2,0,1:T(8,128)(2,1)S(1)} %get-tuple-element.6), channel_id=1, source_target_pairs={{8,0},{16,8},{24,16},{32,24},{40,32},{48,40},{56,48},{64,56},{72,6... | collective-permute-start | bytes 393224 | tf_op jit(solution)/shard_map/ppermute | solution.py:18
  180.4 12.6 %collective-permute-start.14 = (bf16[6,1,8,64,128]{4,3,2,0,1:T(8,128)(2,1)S(1)}, bf16[6,1,8,64,128]{4,3,2,0,1:T(8,128)(2,1)S(1)}, u32[]{:S(2)}, u32[]{:S(2)}) collective-permute-start(bf16[6,1,8,64,128]{4,3,2,0,1:T(8,128)(2,1)S(1)} %pad_maximum_fusion.3), channel_id=1, source_target_pairs={{0,1},{1,2},{2,3},{3,4},{4,5},{5,6},{6,7},{7,0},{8,9},{9,10},{10,1... | collective-permute-start | bytes 2359304 | tf_op jit(solution)/shard_map/ppermute | solution.py:15
  180.5 12.7 %collective-permute-start.15 = (bf16[6,1,8,64,128]{4,3,2,0,1:T(8,128)(2,1)S(1)}, bf16[6,1,8,64,128]{4,3,2,0,1:T(8,128)(2,1)S(1)}, u32[]{:S(2)}, u32[]{:S(2)}) collective-permute-start(bf16[6,1,8,64,128]{4,3,2,0,1:T(8,128)(2,1)S(1)} %pad_maximum_fusion.3), channel_id=1, source_target_pairs={{1,0},{2,1},{3,2},{4,3},{5,4},{6,5},{7,6},{0,7},{9,8},{10,9},{11,1... | collective-permute-start | bytes 2359304 | tf_op jit(solution)/shard_map/ppermute | solution.py:18
  222.6 4.2 %copy-start.2 = (bf16[4,8,128,64]{2,3,1,0:T(8,128)(2,1)S(1)}, bf16[4,8,128,64]{2,3,1,0:T(8,128)(2,1)}, u32[]{:S(2)}) copy-start(bf16[4,8,128,64]{2,3,1,0:T(8,128)(2,1)} %copy-done.1) | copy-start | bytes 1572868
  222.6 4.2 %copy-start.4 = (bf16[4,8,128,64]{2,3,1,0:T(8,128)(2,1)S(1)}, bf16[4,8,128,64]{2,3,1,0:T(8,128)(2,1)}, u32[]{:S(2)}) copy-start(bf16[4,8,128,64]{2,3,1,0:T(8,128)(2,1)} %copy-done.3) | copy-start | bytes 1572868
  222.6 4.2 %copy-start.6 = (bf16[4,8,128,64]{2,3,1,0:T(8,128)(2,1)S(1)}, bf16[4,8,128,64]{2,3,1,0:T(8,128)(2,1)}, u32[]{:S(2)}) copy-start(bf16[4,8,128,64]{2,3,1,0:T(8,128)(2,1)} %copy-done.5) | copy-start | bytes 1572868
where the time goes:
time: 231 us; the launch traced here: 228 us
  local copies, waits for them, and re-layouts  87.4 us (38%)
  waiting for transfers between devices  51.1 us (22%)
  matrix products  50.4 us (22%)
  starting transfers between devices  33.6 us (15%)
  other arithmetic  5.45 us (2%)
    another operation x7, local copies, waits for them, and re-layouts  66.6 us
    ppermute x8, waiting for transfers between devices, with_halo(): lax.ppermute(lax.slice_in_dim(block, block.shape[dim] - width, None, axis...  51.1 us
    dot_general x4, matrix products, apply_rows(): jnp.einsum('jtq,ijqx->ijtx', selector, window, preferred_element_type=jnp...  33.9 us
    ppermute x8, starting transfers between devices, with_halo(): lax.ppermute(lax.slice_in_dim(block, 0, width, axis=dim), axis, backward)  31.7 us
    dot_general x4, matrix products, apply_rows(): jnp.einsum('ijcam,ijcmr->ijcar', blocks, gathered, preferred_element_type...  16.5 us
    another operation x7, local copies, waits for them, and re-layouts, apply_rows(): window = jnp.stack(pieces, axis=2)  11 us
    unnamed x40, local copies, waits for them, and re-layouts  7.83 us
  transfers between devices with their start and end apart: 16, of which 8 were waited for; matrix products, arithmetic and copies ran while one was open for 1% of the time, Pallas kernels for 0%

commit v1 on v0

v1 whole, which is shorter than its diff:
```python
import functools

import jax
import jax.numpy as jnp
from jax import lax
from jax.experimental import pallas as pl
from jax.experimental.pallas import tpu as pltpu
from jax.sharding import PartitionSpec as P

STEPS = 4
MESH = pl.DeviceIdType.MESH


def kernel(
    stream_count, azim_count, columns, faces, couplings,
    neighbour, start_hbm, blocks_hbm, out_hbm,
    vec, blocks, window, from_pair, from_far, from_line, pair_diag, far_diag,
    load_sem, out_sem, pair_s, pair_r, far_s, far_r, line_s, line_r, pd_s, pd_r, fd_s, fd_r,
):
    last = columns - 1
    half = faces // 2
    s = lax.axis_index("stream")
    j = lax.axis_index("azim")
    odd = lax.rem(j, 2)
    pair = {"azim": j + 1 - 2 * odd}
    far = {"azim": lax.rem(j + azim_count - 1 + 2 * odd, azim_count)}
    line = (
        {"stream": lax.rem(s + stream_count - 1, stream_count)},
        {"stream": lax.rem(s + 1, stream_count)},
    )
    pair_slot = 2 - 2 * odd
    far_slot = 2 * odd
    per_column = 3 * faces
    per_window = (columns + 2) * per_column

    load_start = pltpu.make_async_copy(start_hbm, vec.at[0], load_sem.at[0])
    load_blocks = pltpu.make_async_copy(blocks_hbm, blocks, load_sem.at[1])
    load_start.start()
    load_blocks.start()

    barrier = pltpu.get_barrier_semaphore()
    for target in (pair, far, *line):
        pl.semaphore_signal(barrier, inc=1, device_id=target, device_id_type=MESH)
    pl.semaphore_wait(barrier, 4)

    def remote(src, dst, send, recv, target):
        return pltpu.make_async_remote_copy(
            src_ref=src, dst_ref=dst, send_sem=send, recv_sem=recv, device_id=target, device_id_type=MESH
        )

    def far_copy(e, i, h):
        part = pl.ds(i * faces + h * half, half)
        return remote(vec.at[e, part], from_far.at[e, part], far_s.at[e, i, h], far_r.at[e, i, h], far)

    def pair_copy(e, i):
        part = pl.ds(i * faces, faces)
        return remote(vec.at[e, part], from_pair.at[e, part], pair_s.at[e, i], pair_r.at[e, i], pair)

    def line_copy(e, side):
        part = pl.ds(0 if side == 0 else last * faces, faces)
        there = 1 - side
        return remote(vec.at[e, part], from_line.at[e, there], line_s.at[e, there], line_r.at[e, there], line[side])

    def pair_relay(e, side):
        return remote(from_line.at[e, side], pair_diag.at[e, side], pd_s.at[e, side], pd_r.at[e, side], pair)

    def far_relay(e, side, h):
        i = 0 if side == 0 else last
        there = 1 - side
        return remote(
            from_far.at[e, pl.ds(i * faces + h * half, half)],
            far_diag.at[e, there, pl.ds(h * half, half)],
            fd_s.at[e, there, h],
            fd_r.at[e, there, h],
            line[side],
        )

    def fill(parity, position, slot, values):
        at = parity * per_window + position * per_column + slot * faces
        window[pl.ds(at, faces)] = values

    def compute(e, i):
        parity = lax.rem(e, 2)
        base = parity * per_window + i * per_column
        other = (1 - parity) * per_window + (i + 1) * per_column + faces
        for c in range(faces):
            gathered = jnp.concatenate(
                [window[base + neighbour[c * couplings + k]] for k in range(couplings)], axis=0
            )
            value = jnp.dot(
                blocks[i * faces + c], gathered, preferred_element_type=jnp.float32
            ).astype(jnp.bfloat16)
            vec[e + 1, i * faces + c] = value
            window[other + c] = value

    load_start.wait()
    for h in range(2):
        far_copy(0, 0, h).start()
        far_copy(0, last, h).start()
        if h == 0:
            for side in range(2):
                line_copy(0, side).start()
    pair_copy(0, 0).start()
    pair_copy(0, last).start()
    for i in range(1, last):
        for h in range(2):
            far_copy(0, i, h).start()
        pair_copy(0, i).start()
    for i in range(columns):
        fill(0, i + 1, 1, vec[0, pl.ds(i * faces, faces)])
    load_blocks.wait()

    def step(e, carry):
        parity = lax.rem(e, 2)
        more = e < STEPS - 1
        for h in range(2):
            for side in range(2):
                far_copy(e, 0 if side == 0 else last, h).wait_recv()
                far_relay(e, side, h).start()
        for side in range(2):
            line_copy(e, 1 - side).wait_recv()
            pair_relay(e, side).start()
        for i in range(columns):
            pair_copy(e, i).wait_recv()
            fill(parity, i + 1, pair_slot, from_pair[e, pl.ds(i * faces, faces)])
        for i in (0, last):
            fill(parity, i + 1, far_slot, from_far[e, pl.ds(i * faces, faces)])
        for side in range(2):
            fill(parity, side * (columns + 1), 1, from_line[e, side])
        for side in range(2):
            pair_relay(e, side).wait_recv()
            fill(parity, side * (columns + 1), pair_slot, pair_diag[e, side])
        for i in range(1, last):
            for h in range(2):
                far_copy(e, i, h).wait_recv()
            fill(parity, i + 1, far_slot, from_far[e, pl.ds(i * faces, faces)])
        for side in range(2):
            i = 0 if side == 0 else last
            for h in range(2):
                far_relay(e, 1 - side, h).wait_recv()
            fill(parity, side * (columns + 1), far_slot, far_diag[e, side])
            compute(e, i)

            @pl.when(more)
            def _():
                line_copy(e + 1, side).start()
                if side == 0:
                    far_copy(e + 1, 0, 0).start()
                else:
                    far_copy(e + 1, last, 0).start()
                    far_copy(e + 1, 0, 1).start()
                    far_copy(e + 1, last, 1).start()
                pair_copy(e + 1, i).start()

        for i in range(1, last):
            compute(e, i)

            @pl.when(more)
            def _():
                for h in range(2):
                    far_copy(e + 1, i, h).start()
                pair_copy(e + 1, i).start()

        pltpu.make_async_copy(vec.at[e + 1], out_hbm.at[e], out_sem.at[e]).start()
        return carry

    lax.fori_loop(0, STEPS, step, 0)

    def drain(e, carry):
        for i in range(columns):
            for h in range(2):
                far_copy(e, i, h).wait_send()
            pair_copy(e, i).wait_send()
        for side in range(2):
            line_copy(e, side).wait_send()
            pair_relay(e, side).wait_send()
            for h in range(2):
                far_relay(e, side, h).wait_send()
        pltpu.make_async_copy(vec.at[e + 1], out_hbm.at[e], out_sem.at[e]).wait()
        return carry

    lax.fori_loop(0, STEPS, drain, 0)


def solution(mesh):
    stream_count, azim_count = mesh.shape["stream"], mesh.shape["azim"]

    def local(start_vector, trace_blocks, neighbour):
        columns, _, faces, width, rhs = start_vector.shape
        depth = trace_blocks.shape[-1]
        couplings = neighbour.shape[-1]
        total = columns * faces
        slab = (width, rhs)
        bf16 = jnp.bfloat16
        dma = pltpu.SemaphoreType.DMA
        out = pl.pallas_call(
            functools.partial(kernel, stream_count, azim_count, columns, faces, couplings),
            out_shape=jax.ShapeDtypeStruct((STEPS, total, *slab), bf16),
            in_specs=[
                pl.BlockSpec(memory_space=pltpu.SMEM),
                pl.BlockSpec(memory_space=pl.ANY),
                pl.BlockSpec(memory_space=pl.ANY),
            ],
            out_specs=pl.BlockSpec(memory_space=pl.ANY),
            scratch_shapes=[
                pltpu.VMEM((STEPS + 1, total, *slab), bf16),
                pltpu.VMEM((total, width, depth), bf16),
                pltpu.VMEM((2 * (columns + 2) * 3 * faces, *slab), bf16),
                pltpu.VMEM((STEPS, total, *slab), bf16),
                pltpu.VMEM((STEPS, total, *slab), bf16),
                pltpu.VMEM((STEPS, 2, faces, *slab), bf16),
                pltpu.VMEM((STEPS, 2, faces, *slab), bf16),
                pltpu.VMEM((STEPS, 2, faces, *slab), bf16),
                dma((2,)),
                dma((STEPS,)),
                dma((STEPS, columns)),
                dma((STEPS, columns)),
                dma((STEPS, columns, 2)),
                dma((STEPS, columns, 2)),
                dma((STEPS, 2)),
                dma((STEPS, 2)),
                dma((STEPS, 2)),
                dma((STEPS, 2)),
                dma((STEPS, 2, 2)),
                dma((STEPS, 2, 2)),
            ],
            compiler_params=pltpu.CompilerParams(collective_id=0, has_side_effects=True),
        )(
            neighbour.reshape(-1),
            start_vector.reshape(total, *slab),
            trace_blocks.reshape(total, width, depth),
        )
        return out.reshape(STEPS, columns, 1, faces, *slab)

    return jax.shard_map(
        local,
        mesh=mesh,
        in_specs=(
            P("stream", "azim", None, None, None),
            P("stream", "azim", None, None, None),
            P("azim", None, None),
        ),
        out_specs=P(None, "stream", "azim", None, None, None),
        check_vma=False,
    )
```

time: 231 us -> 64.1 us (0.28); the launches traced: 228 us -> 63.9 us
  local copies, waits for them, and re-layouts: 87.4 us -> 4.42 us
  Pallas kernels: 0 us -> 59.5 us
  waiting for transfers between devices: 51.1 us -> 0 us
  matrix products: 50.4 us -> 0 us
  starting transfers between devices: 33.6 us -> 0 us
  other arithmetic: 5.45 us -> 0 us
    another operation x14 -> x0, local copies, waits for them, and re-layouts: 77.6 us -> none
    pallas_call x0 -> x1, Pallas kernels: none -> 59.5 us  [local(): pl.pallas_call(functools.partial(kernel, stream_count, azim_count, column...]
    ppermute x16 -> x0, waiting for transfers between devices: 51.1 us -> none  [the longest x8 51.1 us: with_halo(): lax.ppermute(lax.slice_in_dim(block, block.shape[dim] - width, None, axis...]
    dot_general x8 -> x0, matrix products: 50.4 us -> none  [the longest x4 33.9 us: apply_rows(): jnp.einsum('jtq,ijqx->ijtx', selector, window, preferred_element_type=jnp...]
    ppermute x16 -> x0, starting transfers between devices: 33.6 us -> none  [the longest x8 31.7 us: with_halo(): lax.ppermute(lax.slice_in_dim(block, 0, width, axis=dim), axis, backward)]
    unnamed x40 -> x1, local copies, waits for them, and re-layouts: 7.83 us -> 3.14 us
  transfers between devices with their start and end apart: 16 -> 0, of which waited for: 8 -> 0; matrix products, arithmetic and copies ran while one was open for 1% -> 0% of each run, Pallas kernels for 0% -> 0%
where the time goes in v1:
time: 64.1 us; the launch traced here: 63.9 us
  Pallas kernels  59.5 us (93%)
  local copies, waits for them, and re-layouts  4.42 us (7%)
    pallas_call x1, Pallas kernels, local(): pl.pallas_call(functools.partial(kernel, stream_count, azim_count, column...  59.5 us
    unnamed x1, local copies, waits for them, and re-layouts  3.14 us

profile of v1, /device:TPU:0, one launch (start us, length us, event | category | flops | bytes accessed | tf_op | source)
XLA Modules:
  0.0 63.9 jit_solution(17334969760261662127)
XLA Ops:
  0.0 1.3 %reshape.12.neighbour = s32[96]{0:T(128)} reshape(s32[1,8,12]{2,1,0:T(8,128)} %param.5) | data formatting | bytes 768 | tf_op jit(solution)/shard_map/reshape | solution.py:229
  1.3 59.5 %shard_map.37 = bf16[4,32,64,128]{3,2,1,0:T(8,128)(2,1)} custom-call(s32[96]{0:T(128)} %reshape.12.neighbour, bf16[32,64,128]{2,1,0:T(8,128)(2,1)} %bitcast.7, bf16[32,64,768]{2,1,0:T(8,128)(2,1)} %bitcast.6), custom_call_target="tpu_custom_call" | custom-call | tf_op jit(solution)/shard_map/pallas_call | solution.py:196
  60.8 3.1 %copy.6 = bf16[4,4,1,8,64,128]{5,4,3,2,1,0:T(8,128)(2,1)} copy(bf16[4,4,1,8,64,128]{5,4,3,2,1,0:T(8,128)(2,1)} %bitcast.5) | data formatting | bytes 4194304

commit v2 on v1

v2 whole, which is shorter than its diff:
```python
import functools

import jax
import jax.numpy as jnp
from jax import lax
from jax.experimental import pallas as pl
from jax.experimental.pallas import tpu as pltpu
from jax.sharding import PartitionSpec as P

STEPS = 4
ROW = 4
PARTS = 4
OPT = dict(H=2, order=1, N=4, OUT=2)
MESH = pl.DeviceIdType.MESH


def kernel(
    stream_count, azim_count, columns, faces, couplings,
    neighbour, start_hbm, blocks_hbm, out_hbm,
    vec, blocks, window, from_pair, from_far, from_line, pair_diag, far_diag,
    load_sem, out_sem, pair_s, pair_r, far_s, far_r, line_s, line_r, pd_s, pd_r, fd_s, fd_r,
):
    last = columns - 1
    parts = OPT['H']
    half = faces // parts
    s = lax.axis_index("stream")
    j = lax.axis_index("azim")
    odd = lax.rem(j, 2)
    pair = {"azim": j + 1 - 2 * odd}
    far = {"azim": lax.rem(j + azim_count - 1 + 2 * odd, azim_count)}

    def line(side):
        return {"stream": lax.rem(s + stream_count - 1 + 2 * side, stream_count)}

    first = lax.rem(s, ROW) // 2 if OPT['order'] else 0
    sides = (first, 1 - first)
    pair_slot = 2 - 2 * odd
    far_slot = 2 * odd
    per_column = 3 * faces
    per_window = (columns + 2) * per_column

    load_start = pltpu.make_async_copy(start_hbm, vec.at[0], load_sem.at[0])
    load_blocks = pltpu.make_async_copy(blocks_hbm, blocks, load_sem.at[1])
    load_start.start()
    load_blocks.start()

    barrier = pltpu.get_barrier_semaphore()
    for target in (pair, far, line(0), line(1)):
        pl.semaphore_signal(barrier, inc=1, device_id=target, device_id_type=MESH)
    pl.semaphore_wait(barrier, 4)

    def remote(src, dst, send, recv, target):
        return pltpu.make_async_remote_copy(
            src_ref=src, dst_ref=dst, send_sem=send, recv_sem=recv, device_id=target, device_id_type=MESH
        )

    def far_copy(e, i, h):
        part = pl.ds(i * faces + h * half, half)
        return remote(vec.at[e, part], from_far.at[e, part], far_s.at[e, i, h], far_r.at[e, i, h], far)

    def pair_copy(e, i):
        part = pl.ds(i * faces, faces)
        return remote(vec.at[e, part], from_pair.at[e, part], pair_s.at[e, i], pair_r.at[e, i], pair)

    def line_copy(e, side):
        part = pl.ds(side * last * faces, faces)
        there = 1 - side
        return remote(vec.at[e, part], from_line.at[e, there], line_s.at[e, there], line_r.at[e, there], line(side))

    def pair_relay(e, side):
        return remote(from_line.at[e, side], pair_diag.at[e, side], pd_s.at[e, side], pd_r.at[e, side], pair)

    def far_relay(e, side, h):
        i = side * last
        there = 1 - side
        return remote(
            from_far.at[e, pl.ds(i * faces + h * half, half)],
            far_diag.at[e, there, pl.ds(h * half, half)],
            fd_s.at[e, there, h],
            fd_r.at[e, there, h],
            line(side),
        )

    def fill(parity, position, slot, values):
        at = parity * per_window + position * per_column + slot * faces
        window[pl.ds(at, faces)] = values

    def compute(e, i):
        parity = lax.rem(e, 2)
        base = parity * per_window + i * per_column
        for c in range(faces):
            gathered = jnp.concatenate(
                [window[base + neighbour[0, c, k]] for k in range(couplings)], axis=0
            )
            value = jnp.dot(
                blocks[i * faces + c], gathered, preferred_element_type=jnp.float32
            ).astype(jnp.bfloat16)
            vec[e + 1, i * faces + c] = value
            if OPT['OUT']:
                out_hbm[e, i * faces + c] = value

    def send_edge(e, side):
        for h in range(parts):
            far_copy(e, side * last, h).start()
            if h == 0:
                line_copy(e, side).start()
                pair_copy(e, side * last).start()

    load_start.wait()
    for side in sides:
        send_edge(0, side)
    for i in range(1, last):
        for h in range(parts):
            far_copy(0, i, h).start()
        pair_copy(0, i).start()
    load_blocks.wait()

    def step(e, carry):
        parity = lax.rem(e, 2)
        more = e < OPT['N'] - 1
        for side in sides:
            for h in range(parts):
                far_copy(e, side * last, h).wait_recv()
                far_relay(e, side, h).start()
        for side in sides:
            line_copy(e, 1 - side).wait_recv()
            pair_relay(e, side).start()
        for i in range(columns):
            fill(parity, i + 1, 1, vec[e, pl.ds(i * faces, faces)])
        for i in range(columns):
            pair_copy(e, i).wait_recv()
            fill(parity, i + 1, pair_slot, from_pair[e, pl.ds(i * faces, faces)])
        for i in (0, last):
            fill(parity, i + 1, far_slot, from_far[e, pl.ds(i * faces, faces)])
        for side in range(2):
            fill(parity, side * (columns + 1), 1, from_line[e, side])
        for side in range(2):
            pair_relay(e, side).wait_recv()
            fill(parity, side * (columns + 1), pair_slot, pair_diag[e, side])
        for i in range(1, last):
            for h in range(parts):
                far_copy(e, i, h).wait_recv()
            fill(parity, i + 1, far_slot, from_far[e, pl.ds(i * faces, faces)])
        for side in sides:
            for h in range(parts):
                far_relay(e, 1 - side, h).wait_recv()
            fill(parity, side * (columns + 1), far_slot, far_diag[e, side])
            compute(e, side * last)

            @pl.when(more)
            def _():
                send_edge(e + 1, side)

        for i in range(1, last):
            compute(e, i)

            @pl.when(more)
            def _():
                for h in range(parts):
                    far_copy(e + 1, i, h).start()
                pair_copy(e + 1, i).start()

        if not OPT['OUT']:
            pltpu.make_async_copy(vec.at[e + 1], out_hbm.at[e], out_sem.at[e]).start()
        return carry

    lax.fori_loop(0, OPT['N'], step, 0)

    def drain(e, carry):
        for i in range(columns):
            for h in range(parts):
                far_copy(e, i, h).wait_send()
            pair_copy(e, i).wait_send()
        for side in range(2):
            line_copy(e, side).wait_send()
            pair_relay(e, side).wait_send()
            for h in range(parts):
                far_relay(e, side, h).wait_send()
        if not OPT['OUT']:
            pltpu.make_async_copy(vec.at[e + 1], out_hbm.at[e], out_sem.at[e]).wait()
        return carry

    lax.fori_loop(0, OPT['N'], drain, 0)


def solution(mesh):
    stream_count, azim_count = mesh.shape["stream"], mesh.shape["azim"]

    def local(start_vector, trace_blocks, neighbour):
        columns, _, faces, width, rhs = start_vector.shape
        depth = trace_blocks.shape[-1]
        couplings = neighbour.shape[-1]
        total = columns * faces
        slab = (width, rhs)
        bf16 = jnp.bfloat16
        dma = pltpu.SemaphoreType.DMA
        out = pl.pallas_call(
            functools.partial(kernel, stream_count, azim_count, columns, faces, couplings),
            out_shape=(pltpu.VMEM((STEPS, total, *slab), bf16) if OPT['OUT'] >= 2 else jax.ShapeDtypeStruct((STEPS, total, *slab), bf16)),
            in_specs=[
                pl.BlockSpec(memory_space=pltpu.SMEM),
                pl.BlockSpec(memory_space=pl.ANY),
                pl.BlockSpec(memory_space=pl.ANY),
            ],
            out_specs=pl.BlockSpec(memory_space=pltpu.VMEM if OPT['OUT'] else pl.ANY),
            scratch_shapes=[
                pltpu.VMEM((STEPS + 1, total, *slab), bf16),
                pltpu.VMEM((total, width, depth), bf16),
                pltpu.VMEM((2 * (columns + 2) * 3 * faces, *slab), bf16),
                pltpu.VMEM((STEPS, total, *slab), bf16),
                pltpu.VMEM((STEPS, total, *slab), bf16),
                pltpu.VMEM((STEPS, 2, faces, *slab), bf16),
                pltpu.VMEM((STEPS, 2, faces, *slab), bf16),
                pltpu.VMEM((STEPS, 2, faces, *slab), bf16),
                dma((2,)),
                dma((STEPS,)),
                dma((STEPS, columns)),
                dma((STEPS, columns)),
                dma((STEPS, columns, OPT['H'])),
                dma((STEPS, columns, OPT['H'])),
                dma((STEPS, 2)),
                dma((STEPS, 2)),
                dma((STEPS, 2)),
                dma((STEPS, 2)),
                dma((STEPS, 2, OPT['H'])),
                dma((STEPS, 2, OPT['H'])),
            ],
            compiler_params=pltpu.CompilerParams(collective_id=0, has_side_effects=True),
        )(
            neighbour,
            start_vector.reshape(total, *slab),
            trace_blocks.reshape(total, width, depth),
        )
        if OPT['OUT'] == 3:
            out = pltpu.with_memory_space_constraint(out, pltpu.VMEM)
        if OPT['OUT'] == 3:
            def put(x, o, sem):
                cs = [pltpu.make_async_copy(x.at[t], o.at[t], sem.at[t]) for t in range(STEPS)]
                for c in cs: c.start()
                for c in cs: c.wait()
            out = pl.pallas_call(put, out_shape=jax.ShapeDtypeStruct((STEPS, total, *slab), bf16),
                in_specs=[pl.BlockSpec(memory_space=pltpu.VMEM)], out_specs=pl.BlockSpec(memory_space=pl.ANY),
                scratch_shapes=[dma((STEPS,))])(out)
        return out.reshape(STEPS, columns, 1, faces, *slab)

    return jax.shard_map(
        local,
        mesh=mesh,
        in_specs=(
            P("stream", "azim", None, None, None),
            P("stream", "azim", None, None, None),
            P("azim", None, None),
        ),
        out_specs=P(None, "stream", "azim", None, None, None),
        check_vma=False,
    )
```

time: 64.1 us -> 49.9 us (0.78)
  Pallas kernels: 59.5 us -> 48.4 us
  local copies, waits for them, and re-layouts: 4.42 us -> 1.32 us
    pallas_call x1, Pallas kernels: 59.5 us -> 48.4 us  [local(): pl.pallas_call(functools.partial(kernel, stream_count, azim_count, column...]
    unnamed x1, local copies, waits for them, and re-layouts: 3.14 us -> 1.32 us
    reshape x1 -> x0, local copies, waits for them, and re-layouts: 1.28 us -> none  [local(): neighbour.reshape(-1)]
where the time goes in v2:
time: 49.9 us; the launch traced here: 49.8 us
  Pallas kernels  48.4 us (97%)
  local copies, waits for them, and re-layouts  1.32 us (3%)
    pallas_call x1, Pallas kernels, local(): pl.pallas_call(functools.partial(kernel, stream_count, azim_count, column...  48.4 us
    unnamed x1, local copies, waits for them, and re-layouts  1.32 us

profile of v2, /device:TPU:0, one launch (start us, length us, event | category | flops | bytes accessed | tf_op | source)
XLA Modules:
  0.0 49.8 jit_solution(1168834768640032823)
XLA Ops:
  0.0 48.4 %shard_map.37 = bf16[4,32,64,128]{3,2,1,0:T(8,128)(2,1)S(1)} custom-call(s32[1,8,12]{2,1,0:T(8,128)} %neighbour.1, bf16[32,64,128]{2,1,0:T(8,128)(2,1)} %bitcast.7, bf16[32,64,768]{2,1,0:T(8,128)(2,1)} %bitcast.6), custom_call_target="tpu_custom_call" | custom-call | tf_op jit(solution)/shard_map/pallas_call | solution.py:197
  48.4 1.3 %copy.6 = bf16[4,4,1,8,64,128]{5,4,3,2,1,0:T(8,128)(2,1)} copy(bf16[4,4,1,8,64,128]{5,4,3,2,1,0:T(8,128)(2,1)S(1)} %bitcast.5) | data formatting | bytes 4194304

commit v3 on v2

v3 whole, which is shorter than its diff:
```python
import functools

import jax
import jax.numpy as jnp
from jax import lax
from jax.experimental import pallas as pl
from jax.experimental.pallas import tpu as pltpu
from jax.sharding import PartitionSpec as P

STEPS = 4
ROW = 4
MESH = pl.DeviceIdType.MESH
CUTS = (0, 3, 5)


def kernel(
    stream_count, azim_count, columns, faces, couplings, cuts,
    neighbour, start_hbm, blocks_hbm, out,
    vec, blocks, window, from_pair, from_far, from_line, pair_diag, far_diag,
    load_sem, pair_s, pair_r, far_s, far_r, line_s, line_r, pd_s, pd_r, fd_s, fd_r,
):
    parts = len(cuts) - 1
    last = columns - 1
    s = lax.axis_index("stream")
    j = lax.axis_index("azim")
    odd = lax.rem(j, 2)
    pair = {"azim": j + 1 - 2 * odd}
    far = {"azim": lax.rem(j + azim_count - 1 + 2 * odd, azim_count)}

    def line(side):
        return {"stream": lax.rem(s + stream_count - 1 + 2 * side, stream_count)}

    place = lax.rem(s, ROW)
    first = place // 2
    sides = (first, 1 - first)
    at_end = lax.rem(place, ROW - 1) == 0
    pair_slot = 2 - 2 * odd
    inner = (1 + first * (columns - 3), columns - 2 - first * (columns - 3))
    far_slot = 2 * odd
    per_column = 3 * faces
    per_window = (columns + 2) * per_column

    load_start = pltpu.make_async_copy(start_hbm, vec.at[0], load_sem.at[0])
    load_blocks = pltpu.make_async_copy(blocks_hbm, blocks, load_sem.at[1])
    load_start.start()

    barrier = pltpu.get_barrier_semaphore()
    for target in (pair, far, line(0), line(1)):
        pl.semaphore_signal(barrier, inc=1, device_id=target, device_id_type=MESH)
    pl.semaphore_wait(barrier, 4)

    def remote(src, dst, send, recv, target):
        return pltpu.make_async_remote_copy(
            src_ref=src, dst_ref=dst, send_sem=send, recv_sem=recv, device_id=target, device_id_type=MESH
        )

    def far_copy(e, i, h):
        part = pl.ds(i * faces + cuts[h], cuts[h + 1] - cuts[h])
        return remote(vec.at[e, part], from_far.at[e, part], far_s.at[e, i, h], far_r.at[e, i, h], far)

    def far_whole(e, i):
        part = pl.ds(i * faces, faces)
        return remote(vec.at[e, part], from_far.at[e, part], far_s.at[e, i, 0], far_r.at[e, i, 0], far)

    def pair_copy(e, i):
        part = pl.ds(i * faces, faces)
        return remote(vec.at[e, part], from_pair.at[e, part], pair_s.at[e, i], pair_r.at[e, i], pair)

    def line_copy(e, side, piece):
        begin, end = (cuts[-2], faces) if piece == 0 else (0, cuts[-2])
        there = 1 - side
        return remote(
            vec.at[e, pl.ds(side * last * faces + begin, end - begin)],
            from_line.at[e, there, pl.ds(begin, end - begin)],
            line_s.at[e, there, piece],
            line_r.at[e, there, piece],
            line(side),
        )

    def pair_relay(e, side):
        return remote(from_line.at[e, side], pair_diag.at[e, side], pd_s.at[e, side], pd_r.at[e, side], pair)

    def far_relay(e, side, h):
        there = 1 - side
        size = cuts[h + 1] - cuts[h]
        return remote(
            from_far.at[e, pl.ds(side * last * faces + cuts[h], size)],
            far_diag.at[e, there, pl.ds(cuts[h], size)],
            fd_s.at[e, there, h],
            fd_r.at[e, there, h],
            line(side),
        )

    def end_relay(e, side):
        h = parts - 1
        part = pl.ds(cuts[h], cuts[h + 1] - cuts[h])
        return remote(
            from_line.at[e, side, part],
            far_diag.at[e, side, part],
            fd_s.at[e, 1 - side, h],
            fd_r.at[e, side, h],
            far,
        )

    def send_edge(e, side):
        for h in range(parts):
            far_copy(e, side * last, h).start()
            if h == 0:
                line_copy(e, side, 0).start()
                line_copy(e, side, 1).start()
                pair_copy(e, side * last).start()

    def send_inner(e, i):
        far_whole(e, i).start()
        pair_copy(e, i).start()

    def fill(parity, position, slot, values):
        at = parity * per_window + position * per_column + slot * faces
        window[pl.ds(at, faces)] = values

    def compute(e, i):
        base = lax.rem(e, 2) * per_window + i * per_column
        for c in range(faces):
            f = i * faces + c
            gathered = jnp.concatenate(
                [window[base + neighbour[0, c, k]] for k in range(couplings)], axis=0
            )
            value = jnp.dot(
                blocks[f], gathered, preferred_element_type=jnp.float32
            ).astype(jnp.bfloat16)
            vec[e + 1, f] = value
            out[e, f] = value

    load_start.wait()
    load_blocks.start()
    for side in sides:
        send_edge(0, side)
    for i in inner:
        send_inner(0, i)
    load_blocks.wait()

    def step(e, final):
        parity = lax.rem(e, 2)
        for n, side in enumerate(sides):
            for h in range(parts):
                far_copy(e, side * last, h).wait_recv()
                if n == 0 and h == parts - 1:

                    @pl.when(jnp.logical_not(at_end))
                    def _():
                        far_relay(e, side, h).start()

                else:
                    far_relay(e, side, h).start()
            if n == 0:
                line_copy(e, 1 - sides[0], 0).wait_recv()

                @pl.when(at_end)
                def _():
                    end_relay(e, sides[0]).start()

        for n in (1, 0):
            side = sides[n]
            if n == 1:
                line_copy(e, 1 - side, 0).wait_recv()
            line_copy(e, 1 - side, 1).wait_recv()
            pair_relay(e, side).start()
        for i in range(columns):
            fill(parity, i + 1, 1, vec[e, pl.ds(i * faces, faces)])
        for i in range(columns):
            pair_copy(e, i).wait_recv()
            fill(parity, i + 1, pair_slot, from_pair[e, pl.ds(i * faces, faces)])
        for i in (0, last):
            fill(parity, i + 1, far_slot, from_far[e, pl.ds(i * faces, faces)])
        for side in range(2):
            fill(parity, side * (columns + 1), 1, from_line[e, side])
        for i in inner:
            far_whole(e, i).wait_recv()
            fill(parity, i + 1, far_slot, from_far[e, pl.ds(i * faces, faces)])
        if final:
            for i in inner:
                compute(e, i)
        for side in range(2):
            pair_relay(e, side).wait_recv()
            fill(parity, side * (columns + 1), pair_slot, pair_diag[e, side])
        for side in sides:
            for h in range(parts):
                far_relay(e, 1 - side, h).wait_recv()
            fill(parity, side * (columns + 1), far_slot, far_diag[e, side])
            compute(e, side * last)
            if not final:
                send_edge(e + 1, side)
        if not final:
            for i in inner:
                compute(e, i)
                send_inner(e + 1, i)

    def middle(e, carry):
        step(e, False)
        return carry

    lax.fori_loop(0, STEPS - 1, middle, 0)
    step(STEPS - 1, True)

    def drain(e, carry):
        for i in range(columns):
            pair_copy(e, i).wait_send()
        for i in inner:
            far_whole(e, i).wait_send()
        for side in range(2):
            for piece in range(2):
                line_copy(e, side, piece).wait_send()
            pair_relay(e, side).wait_send()
            for h in range(parts):
                far_copy(e, side * last, h).wait_send()
                far_relay(e, side, h).wait_send()
        return carry

    lax.fori_loop(0, STEPS, drain, 0)


def solution(mesh):
    stream_count, azim_count = mesh.shape["stream"], mesh.shape["azim"]

    def local(start_vector, trace_blocks, neighbour):
        columns, _, faces, width, rhs = start_vector.shape
        depth = trace_blocks.shape[-1]
        couplings = neighbour.shape[-1]
        total = columns * faces
        slab = (width, rhs)
        bf16 = jnp.bfloat16
        dma = pltpu.SemaphoreType.DMA
        cuts = (*CUTS, faces)
        parts = len(cuts) - 1
        out = pl.pallas_call(
            functools.partial(kernel, stream_count, azim_count, columns, faces, couplings, cuts),
            out_shape=pltpu.VMEM((STEPS, total, *slab), bf16),
            in_specs=[
                pl.BlockSpec(memory_space=pltpu.SMEM),
                pl.BlockSpec(memory_space=pl.ANY),
                pl.BlockSpec(memory_space=pl.ANY),
            ],
            out_specs=pl.BlockSpec(memory_space=pltpu.VMEM),
            scratch_shapes=[
                pltpu.VMEM((STEPS + 1, total, *slab), bf16),
                pltpu.VMEM((total, width, depth), bf16),
                pltpu.VMEM((2 * (columns + 2) * 3 * faces, *slab), bf16),
                pltpu.VMEM((STEPS, total, *slab), bf16),
                pltpu.VMEM((STEPS, total, *slab), bf16),
                pltpu.VMEM((STEPS, 2, faces, *slab), bf16),
                pltpu.VMEM((STEPS, 2, faces, *slab), bf16),
                pltpu.VMEM((STEPS, 2, faces, *slab), bf16),
                dma((2,)),
                dma((STEPS, columns)),
                dma((STEPS, columns)),
                dma((STEPS, columns, parts)),
                dma((STEPS, columns, parts)),
                dma((STEPS, 2, 2)),
                dma((STEPS, 2, 2)),
                dma((STEPS, 2)),
                dma((STEPS, 2)),
                dma((STEPS, 2, parts)),
                dma((STEPS, 2, parts)),
            ],
            compiler_params=pltpu.CompilerParams(collective_id=0, has_side_effects=True),
        )(
            neighbour,
            start_vector.reshape(total, *slab),
            trace_blocks.reshape(total, width, depth),
        )
        return out.reshape(STEPS, columns, 1, faces, *slab)

    return jax.shard_map(
        local,
        mesh=mesh,
        in_specs=(
            P("stream", "azim", None, None, None),
            P("stream", "azim", None, None, None),
            P("azim", None, None),
        ),
        out_specs=P(None, "stream", "azim", None, None, None),
        check_vma=False,
    )
```

time: 49.9 us -> 48.5 us (0.972)
  Pallas kernels: 48.4 us -> 47 us
    pallas_call x1, Pallas kernels: 48.4 us -> 47 us  [local(): pl.pallas_call(functools.partial(kernel, stream_count, azim_count, column...]
where the time goes in v3:
time: 48.5 us; the launch traced here: 48.3 us
  Pallas kernels  47 us (97%)
  local copies, waits for them, and re-layouts  1.32 us (3%)
    pallas_call x1, Pallas kernels, local(): pl.pallas_call(functools.partial(kernel, stream_count, azim_count, column...  47 us
    unnamed x1, local copies, waits for them, and re-layouts  1.32 us

profile of v3, /device:TPU:0, one launch (start us, length us, event | category | flops | bytes accessed | tf_op | source)
XLA Modules:
  0.0 48.3 jit_solution(17444699664792555240)
XLA Ops:
  0.0 47.0 %shard_map.37 = bf16[4,32,64,128]{3,2,1,0:T(8,128)(2,1)S(1)} custom-call(s32[1,8,12]{2,1,0:T(8,128)} %neighbour.1, bf16[32,64,128]{2,1,0:T(8,128)(2,1)} %bitcast.7, bf16[32,64,768]{2,1,0:T(8,128)(2,1)} %bitcast.6), custom_call_target="tpu_custom_call" | custom-call | tf_op jit(solution)/shard_map/pallas_call | solution.py:235
  47.0 1.3 %copy.6 = bf16[4,4,1,8,64,128]{5,4,3,2,1,0:T(8,128)(2,1)} copy(bf16[4,4,1,8,64,128]{5,4,3,2,1,0:T(8,128)(2,1)S(1)} %bitcast.5) | data formatting | bytes 4194304
